TPU v7x, 32 devices: a whole 2x2x4 slice. The times are simulated.
32 devices in a mesh: row: 8 (over y, x, core), col: 4 (over z).
Axes of the slice: x: 2, y: 2, z: 4, core: 2. Of those that a mesh axis runs over, the one named last changes fastest.
Arguments:
- design: bfloat16 [512, 90112], P(('row', 'col')), may hold values from -6 to 6
- arc_partials: float32 [32, 6, 16], P(('row', 'col')), may hold values from -6 to 6
- arc_id: int32 [32], P(('row', 'col')), may hold values from 0 to 7
- arc_weight: float32 [8], replicated, may hold values from 0.25 to 4
Outputs:
- normal_slab: float32 [90112, 2048], P('row', 'col')
All inputs are finite; a program needn't handle non-finite values.
Results may differ from a plain program's by a relative error of at most 0.0003.
The roundings to bfloat16 on the way count: a program that leaves them out, or rounds other values in their place, can miss the bound.
Values may be sent and summed in bfloat16 or wider, within the bound.
A program may use at most 128 MiB of HBM per device.

v0:
```python
import jax
import jax.numpy as jnp
from jax import lax
from jax.sharding import PartitionSpec as P

SLAB = 2048
ridge = 4.0


def solve_small(matrix, rhs):
    order = matrix.shape[-1]
    for pivot in range(order):
        scale = 1.0 / matrix[..., pivot, pivot]
        row_mat = matrix[..., pivot, :] * scale[..., None]
        row_rhs = rhs[..., pivot, :] * scale[..., None]
        factor = matrix[..., :, pivot]
        matrix = matrix - factor[..., :, None] * row_mat[..., None, :]
        rhs = rhs - factor[..., :, None] * row_rhs[..., None, :]
        matrix = matrix.at[..., pivot, :].set(row_mat)
        rhs = rhs.at[..., pivot, :].set(row_rhs)
    return rhs


def own_reduced(design, arc_partials, arc_id, arc_weight):
    high = lax.Precision.HIGHEST
    slab_rows = design[:, :SLAB].astype(jnp.float32)
    partials = arc_partials[0]
    coupling = jnp.dot(partials, slab_rows, precision=high, preferred_element_type=jnp.float32)
    gram = jnp.dot(partials, partials.T, precision=high, preferred_element_type=jnp.float32)
    arc_count = arc_weight.shape[0]
    select = (jnp.arange(arc_count) == arc_id[0]).astype(jnp.float32)
    arc_gram, arc_coupling = lax.psum(
        (select[:, None, None] * gram[None], select[:, None, None] * coupling[None]), ("row", "col")
    )
    order = partials.shape[0]
    own_gram = jnp.sum(select[:, None, None] * arc_gram, axis=0) + ridge * jnp.eye(
        order, dtype=jnp.float32
    )
    own_coupling = jnp.sum(select[:, None, None] * arc_coupling, axis=0)
    solved = solve_small(own_gram, own_coupling)
    reduced = slab_rows - jnp.dot(
        partials.T, solved, precision=high, preferred_element_type=jnp.float32
    )
    weight = jnp.sum(select * arc_weight)
    return (weight * reduced).astype(jnp.bfloat16)


def make_accumulate(ordered, piece):
    return lax.dot_general(
        piece, ordered, (((0,), (0,)), ((), ())), preferred_element_type=jnp.float32
    )


def col_major(slab_global, row_count, col_count, rows_dev):
    width = slab_global.shape[1]
    ordered = slab_global.reshape(row_count, col_count, rows_dev, width)
    return ordered.transpose(1, 0, 2, 3).reshape(rows_dev * row_count * col_count, width)


def local(design, arc_partials, arc_id, arc_weight):
    rows_dev = design.shape[0]
    row_count = lax.axis_size("row")
    col_count = lax.axis_size("col")
    devices = row_count * col_count
    epochs = rows_dev * devices
    eliminated_own = own_reduced(design, arc_partials, arc_id, arc_weight)
    regrouped = lax.all_to_all(design, "row", split_axis=1, concat_axis=0, tiled=True)
    columns = lax.all_to_all(eliminated_own, "col", split_axis=1, concat_axis=0, tiled=True)
    slab_global = lax.all_gather(columns, "row", axis=0, tiled=True)
    ordered = col_major(slab_global, row_count, col_count, rows_dev)
    normal = make_accumulate(ordered, lax.all_gather(regrouped, "col", axis=0, tiled=True))
    return normal * (1.0 / epochs)


def solution(mesh):
    placed = (P(("row", "col"), None), P(("row", "col"), None, None), P(("row", "col")), P())
    return jax.shard_map(
        local, mesh=mesh, in_specs=placed, out_specs=P("row", "col"), check_vma=False
    )
```

profile of v0, /device:TPU:0, one launch (start us, length us, event | category | flops | bytes accessed | tf_op | source)
XLA Modules:
  0.0 400.1 jit_solution(14108734418693655313)
XLA Ops:
  7.4 3.6 copy.42
  11.0 5.2 %all-to-all-start.1 = ((bf16[16,8,11264]{2,0,1:T(8,128)(2,1)}), bf16[16,8,11264]{2,0,1:T(8,128)(2,1)S(1)}, u32[]{:S(2)}, u32[]{:S(2)}) async-start(bf16[16,8,11264]{2,0,1:T(8,128)(2,1)} %bitcast.64), calls=%async_computation.1 | async-start | bytes 5767168 | tf_op jit(solution)/shard_map/all_to_all | solution.py:67
  16.9 1.0 fusion.3
  17.9 0.8 broadcast_multiply_fusion
  18.8 33.2 %all-to-all-done.1 = bf16[16,8,11264]{2,0,1:T(8,128)(2,1)S(1)} async-done(((bf16[16,8,11264]{2,0,1:T(8,128)(2,1)}), bf16[16,8,11264]{2,0,1:T(8,128)(2,1)S(1)}, u32[]{:S(2)}, u32[]{:S(2)}) %all-to-all-start.1) | async-done | bytes 2883616 | tf_op jit(solution)/shard_map/all_to_all | solution.py:67
  52.0 1.6 copy-done
  53.8 50.2 %psum.15 = f32[8,6,6]{2,0,1:T(8,128)S(1)} all-reduce(f32[8,6,6]{2,0,1:T(8,128)S(1)} %broadcast_multiply_fusion.1), channel_id=1, replica_groups=mesh['row'=8,'col'=4] {'row','col'}, use_global_device_ids=true, to_apply=%region_3.0 | all-reduce | flops 288 | bytes 2304 | tf_op jit(solution)/shard_map/psum | solution.py:32
  104.1 0.5 slice.240
  105.5 0.6 slice.244
  106.8 0.2 slice_reduce_fusion.4
  107.1 0.6 slice.248
  108.4 0.2 slice_reduce_fusion.3
  108.7 0.6 slice.252
  110.0 0.2 slice_reduce_fusion.2
  110.3 0.6 slice.256
  111.5 0.2 slice_reduce_fusion.1
  111.8 0.6 slice.260
  113.2 0.6 fusion.12
  113.8 0.2 slice_reduce_fusion
  114.0 216.3 %all-reduce.2.cloned.1.call-done = f32[8,6,2048]{2,0,1:T(8,128)} async-done(((f32[8,6,2048]{2,0,1:T(8,128)}), f32[8,6,2048]{2,0,1:T(8,128)}) %all-reduce.2.cloned.1.call-update) | async-done | bytes 393232 | tf_op jit(solution)/shard_map/psum | solution.py:32
  330.3 1.2 multiply_reduce_fusion
  331.6 0.2 scatter.36
  331.9 0.2 scatter.40
  332.1 0.2 scatter.44
  332.4 0.2 scatter.46
  332.7 0.2 scatter.50
  333.0 0.2 scatter.54
  333.2 1.7 fusion.2
  334.9 9.2 %all_to_all.38 = bf16[16,4,512]{2,0,1:T(8,128)(2,1)S(1)} all-to-all(bf16[16,4,512]{2,0,1:T(8,128)(2,1)S(1)} %bitcast.70), channel_id=1, replica_groups=mesh['row'=8,'col'=4] {'col'}, dimensions={1} | all-to-all | bytes 131072 | tf_op jit(solution)/shard_map/all_to_all | solution.py:68
  344.1 9.8 %all_gather.6 = bf16[512,512]{1,0:T(8,128)(2,1)S(1)} all-gather(bf16[64,512]{1,0:T(8,128)(2,1)S(1)} %bitcast.69), channel_id=1, replica_groups=mesh['row'=8,'col'=4] {'row'}, dimensions={0}, use_global_device_ids=true | all-gather | bytes 589824 | tf_op jit(solution)/shard_map/all_gather | solution.py:69
  354.0 15.2 %multiply_bitcast_fusion = f32[11264,512]{0,1:T(8,128)} fusion(bf16[512,512]{1,0:T(8,128)(2,1)S(1)} %bitcast.65, bf16[512,11264]{1,0:T(8,128)(2,1)} %all-gather.2.cloned.1.call-done), kind=kOutput, calls=%fused_computation | convolution fusion | flops 5911347200 | bytes 35127296 | tf_op jit(solution)/shard_map/dot_general | solution.py:49
  369.1 23.5 %copy.24 = f32[11264,512]{1,0:T(8,128)} copy(f32[11264,512]{0,1:T(8,128)} %multiply_bitcast_fusion) | data formatting | bytes 46137344 | tf_op jit(solution)/shard_map/mul | solution.py:72
  (50 shorter events, 1.7 us)
Async XLA Ops:
  7.4 9.5 %copy-start.1 = (f32[1,6,16]{2,0,1:T(1,128)S(1)}, f32[1,6,16]{2,0,1:T(1,128)}, u32[]{:S(2)}) copy-start(f32[1,6,16]{2,0,1:T(1,128)} %param.27) | copy-start | bytes 1156
  7.4 105.8 %copy-start.2 = (f32[8]{0:T(128)S(1)}, f32[8]{0:T(128)}, u32[]{:S(2)}) copy-start(f32[8]{0:T(128)} %param.29) | copy-start | bytes 100
  11.0 41.0 %all-to-all-start.1 = ((bf16[16,8,11264]{2,0,1:T(8,128)(2,1)}), bf16[16,8,11264]{2,0,1:T(8,128)(2,1)S(1)}, u32[]{:S(2)}, u32[]{:S(2)}) async-start(bf16[16,8,11264]{2,0,1:T(8,128)(2,1)} %bitcast.64), calls=%async_computation.1 | async-start | bytes 5767168 | tf_op jit(solution)/shard_map/all_to_all | solution.py:67
  16.2 314.1 %all-reduce.2.cloned.1.call-start = ((), (), s32[]{:S(2)}) async-start(), calls=%async_computation.2 | async-start | bytes 786432 | tf_op jit(solution)/shard_map/psum | solution.py:32
  18.8 335.2 %all-gather.2.cloned.1.call-start = ((), (), s32[]{:S(2)}) async-start(), calls=%async_computation.3 | async-start | bytes 14417920 | tf_op jit(solution)/shard_map/all_gather | solution.py:71
  52.0 1.6 copy-start
Sparse Core Ops, SparseCore 0:
  22.3 307.9 all-reduce.1
Sparse Core Ops, SparseCore 1:
  53.7 201.6 all-gather.1
where the time goes:
time: 401 us; the launch traced here: 400 us
  waiting for transfers between devices  250 us (62%)
  blocking collectives  69.1 us (17%)
  local copies, waits for them, and re-layouts  34.6 us (9%)
  between operations  19.7 us (5%)
  matrix products  18 us (4%)
  starting transfers between devices  5.28 us (1%)
    psum x1, waiting for transfers between devices, own_reduced(): lax.psum((select[:, None, None] * gram[None], select[:, None, None] * cou...  216 us
    psum x1, blocking collectives, own_reduced(): lax.psum((select[:, None, None] * gram[None], select[:, None, None] * cou...  50.2 us
    all_to_all x1, waiting for transfers between devices, local(): lax.all_to_all(design, 'row', split_axis=1, concat_axis=0, tiled=True)  33.2 us
    mul x1, local copies, waits for them, and re-layouts, local(): return normal * (1.0 / epochs)  23.5 us
    dot_general x1, matrix products, make_accumulate(): lax.dot_general(piece, ordered, (((0,), (0,)), ((), ())), preferred_eleme...  15.2 us
    all_gather x1, blocking collectives, local(): slab_global = lax.all_gather(columns, 'row', axis=0, tiled=True)  9.79 us
    all_to_all x1, blocking collectives, local(): lax.all_to_all(eliminated_own, 'col', split_axis=1, concat_axis=0, tiled=...  9.18 us
  transfers between devices with their start and end apart: 3, of which 2 were waited for; matrix products, arithmetic and copies ran while one was open for 3% of the time, Pallas kernels for 0%

commit v1 on v0

--- a/solution.py
+++ b/solution.py
@@ -5,6 +5,11 @@
 
 SLAB = 2048
 ridge = 4.0
+
+
+def by_each_axis(value, inner_axis, outer_axis):
+    half = lax.psum(value, inner_axis)
+    return lax.psum(half, outer_axis)
 
 
 def solve_small(matrix, rhs):
@@ -29,8 +34,8 @@
     gram = jnp.dot(partials, partials.T, precision=high, preferred_element_type=jnp.float32)
     arc_count = arc_weight.shape[0]
     select = (jnp.arange(arc_count) == arc_id[0]).astype(jnp.float32)
-    arc_gram, arc_coupling = lax.psum(
-        (select[:, None, None] * gram[None], select[:, None, None] * coupling[None]), ("row", "col")
+    arc_gram, arc_coupling = by_each_axis(
+        (select[:, None, None] * gram[None], select[:, None, None] * coupling[None]), "col", "row"
     )
     order = partials.shape[0]
     own_gram = jnp.sum(select[:, None, None] * arc_gram, axis=0) + ridge * jnp.eye(

time: 401 us -> 363 us (0.905)
  waiting for transfers between devices: 250 us -> 223 us
  blocking collectives: 69.1 us -> 59.3 us
    all_gather x1, waiting for transfers between devices: 0.03 us -> 178 us  [local(): lax.all_gather(regrouped, 'col', axis=0, tiled=True)]
    psum x1 -> x2, waiting for transfers between devices: 216 us -> 44.6 us  [the longest x1 39.3 us: by_each_axis(): half = lax.psum(value, inner_axis)]
    all_to_all x1, waiting for transfers between devices: 33.2 us -> 0.01 us  [local(): lax.all_to_all(design, 'row', split_axis=1, concat_axis=0, tiled=True)]
    psum x1 -> x2, blocking collectives: 50.2 us -> 40 us  [the longest x1 22.4 us: by_each_axis(): return lax.psum(half, outer_axis)]
  transfers between devices with their start and end apart: 3 -> 4, of which waited for: 2 -> 3; matrix products, arithmetic and copies ran while one was open for 3% -> 3% of each run, Pallas kernels for 0% -> 0%
where the time goes in v1:
time: 363 us; the launch traced here: 362 us
  waiting for transfers between devices  223 us (61%)
  blocking collectives  59.3 us (16%)
  local copies, waits for them, and re-layouts  34.6 us (10%)
  matrix products  18 us (5%)
  between operations  18 us (5%)
  starting transfers between devices  5.31 us (1%)
  other arithmetic  3.7 us (1%)
    all_gather x1, waiting for transfers between devices, local(): lax.all_gather(regrouped, 'col', axis=0, tiled=True)  178 us
    psum x1, waiting for transfers between devices, by_each_axis(): half = lax.psum(value, inner_axis)  39.3 us
    mul x1, local copies, waits for them, and re-layouts, local(): return normal * (1.0 / epochs)  23.5 us
    psum x1, blocking collectives, by_each_axis(): return lax.psum(half, outer_axis)  22.4 us
    psum x1, blocking collectives, by_each_axis(): half = lax.psum(value, inner_axis)  17.7 us
    dot_general x1, matrix products, make_accumulate(): lax.dot_general(piece, ordered, (((0,), (0,)), ((), ())), preferred_eleme...  15.2 us
    all_to_all x1, blocking collectives, local(): lax.all_to_all(eliminated_own, 'col', split_axis=1, concat_axis=0, tiled=...  10.3 us
    all_gather x1, blocking collectives, local(): slab_global = lax.all_gather(columns, 'row', axis=0, tiled=True)  8.99 us
  transfers between devices with their start and end apart: 4, of which 3 were waited for; matrix products, arithmetic and copies ran while one was open for 3% of the time, Pallas kernels for 0%

profile of v1, /device:TPU:0, one launch (start us, length us, event | category | flops | bytes accessed | tf_op | source)
XLA Modules:
  0.0 361.7 jit_solution(6462691683170628908)
XLA Ops:
  6.5 3.6 copy.42
  10.1 5.2 %all-to-all-start.1 = ((bf16[16,8,11264]{2,0,1:T(8,128)(2,1)}), bf16[16,8,11264]{2,0,1:T(8,128)(2,1)S(1)}, u32[]{:S(2)}, u32[]{:S(2)}) async-start(bf16[16,8,11264]{2,0,1:T(8,128)(2,1)} %bitcast.64), calls=%async_computation.1 | async-start | bytes 5767168 | tf_op jit(solution)/shard_map/all_to_all | solution.py:72
  16.1 1.0 fusion.3
  17.1 0.8 broadcast_multiply_fusion
  18.0 39.3 %all-reduce.3.cloned.1.call-done = f32[8,6,2048]{2,0,1:T(8,128)} async-done(((f32[8,6,2048]{2,0,1:T(8,128)}), f32[8,6,2048]{2,0,1:T(8,128)}) %all-reduce.3.cloned.1.call-update) | async-done | bytes 393232 | tf_op jit(solution)/shard_map/psum | solution.py:11
  57.4 1.6 copy-done
  59.2 17.7 %psum.30 = f32[8,6,6]{2,0,1:T(8,128)S(1)} all-reduce(f32[8,6,6]{2,0,1:T(8,128)S(1)} %broadcast_multiply_fusion.1), channel_id=1, replica_groups=mesh['row'=8,'col'=4] {'col'}, use_global_device_ids=true, to_apply=%region_4.0 | all-reduce | flops 288 | bytes 2304 | tf_op jit(solution)/shard_map/psum | solution.py:11
  76.9 22.4 %psum.31 = f32[8,6,6]{2,0,1:T(8,128)S(1)} all-reduce(f32[8,6,6]{2,0,1:T(8,128)S(1)} %psum.30), channel_id=1, replica_groups=mesh['row'=8,'col'=4] {'row'}, use_global_device_ids=true, to_apply=%region_5.0 | all-reduce | flops 288 | bytes 2304 | tf_op jit(solution)/shard_map/psum | solution.py:12
  99.3 0.5 slice.240
  100.8 0.6 slice.244
  102.1 0.2 slice_reduce_fusion.4
  102.4 0.6 slice.248
  103.7 0.2 slice_reduce_fusion.3
  104.0 0.6 slice.252
  105.3 0.2 slice_reduce_fusion.2
  105.6 0.6 slice.256
  107.1 0.6 slice.260
  108.5 0.6 fusion.12
  109.2 5.3 %all-reduce.5.cloned.1.call-done = f32[8,6,2048]{2,0,1:T(8,128)} async-done(((f32[8,6,2048]{2,0,1:T(8,128)}), f32[8,6,2048]{2,0,1:T(8,128)}) %all-reduce.5.cloned.1.call-update) | async-done | bytes 393232 | tf_op jit(solution)/shard_map/psum | solution.py:12
  114.5 1.2 multiply_reduce_fusion
  115.8 0.2 scatter.36
  116.1 0.2 scatter.40
  116.3 0.2 scatter.44
  116.6 0.2 scatter.46
  116.9 0.2 scatter.50
  117.2 0.2 scatter.54
  117.4 1.7 fusion.2
  119.1 10.3 %all_to_all.38 = bf16[16,4,512]{2,0,1:T(8,128)(2,1)S(1)} all-to-all(bf16[16,4,512]{2,0,1:T(8,128)(2,1)S(1)} %bitcast.70), channel_id=1, replica_groups=mesh['row'=8,'col'=4] {'col'}, dimensions={1} | all-to-all | bytes 131072 | tf_op jit(solution)/shard_map/all_to_all | solution.py:73
  129.4 9.0 %all_gather.6 = bf16[512,512]{1,0:T(8,128)(2,1)S(1)} all-gather(bf16[64,512]{1,0:T(8,128)(2,1)S(1)} %bitcast.69), channel_id=1, replica_groups=mesh['row'=8,'col'=4] {'row'}, dimensions={0}, use_global_device_ids=true | all-gather | bytes 589824 | tf_op jit(solution)/shard_map/all_gather | solution.py:74
  138.4 178.1 %all-gather.2.cloned.1.call-done = bf16[512,11264]{1,0:T(8,128)(2,1)} async-done(((bf16[128,11264]{1,0:T(8,128)(2,1)}), bf16[512,11264]{1,0:T(8,128)(2,1)}) %all-gather.2.cloned.1.call-update) | async-done | bytes 11534352 | tf_op jit(solution)/shard_map/all_gather | solution.py:76
  316.5 15.2 %multiply_bitcast_fusion = f32[11264,512]{0,1:T(8,128)} fusion(bf16[512,512]{1,0:T(8,128)(2,1)S(1)} %bitcast.65, bf16[512,11264]{1,0:T(8,128)(2,1)} %all-gather.2.cloned.1.call-done), kind=kOutput, calls=%fused_computation | convolution fusion | flops 5911347200 | bytes 35127296 | tf_op jit(solution)/shard_map/dot_general | solution.py:54
  331.7 23.5 %copy.24 = f32[11264,512]{1,0:T(8,128)} copy(f32[11264,512]{0,1:T(8,128)} %multiply_bitcast_fusion) | data formatting | bytes 46137344 | tf_op jit(solution)/shard_map/mul | solution.py:77
  (54 shorter events, 2.1 us)
Async XLA Ops:
  6.5 9.5 %copy-start.1 = (f32[1,6,16]{2,0,1:T(1,128)S(1)}, f32[1,6,16]{2,0,1:T(1,128)}, u32[]{:S(2)}) copy-start(f32[1,6,16]{2,0,1:T(1,128)} %param.27) | copy-start | bytes 1156
  6.5 101.9 %copy-start.2 = (f32[8]{0:T(128)S(1)}, f32[8]{0:T(128)}, u32[]{:S(2)}) copy-start(f32[8]{0:T(128)} %param.29) | copy-start | bytes 100
  10.1 47.2 %all-to-all-start.1 = ((bf16[16,8,11264]{2,0,1:T(8,128)(2,1)}), bf16[16,8,11264]{2,0,1:T(8,128)(2,1)S(1)}, u32[]{:S(2)}, u32[]{:S(2)}) async-start(bf16[16,8,11264]{2,0,1:T(8,128)(2,1)} %bitcast.64), calls=%async_computation.1 | async-start | bytes 5767168 | tf_op jit(solution)/shard_map/all_to_all | solution.py:72
  15.3 42.0 %all-reduce.3.cloned.1.call-start = ((), (), s32[]{:S(2)}) async-start(), calls=%async_computation.2 | async-start | bytes 786432 | tf_op jit(solution)/shard_map/psum | solution.py:11
  17.9 96.6 %all-reduce.5.cloned.1.call-start = ((), (), s32[]{:S(2)}) async-start(), calls=%async_computation.3 | async-start | bytes 786432 | tf_op jit(solution)/shard_map/psum | solution.py:12
  57.3 259.2 %all-gather.2.cloned.1.call-start = ((), (), s32[]{:S(2)}) async-start(), calls=%async_computation.4 | async-start | bytes 14417920 | tf_op jit(solution)/shard_map/all_gather | solution.py:76
  57.4 1.6 copy-start
Sparse Core Ops, SparseCore 0:
  18.5 38.7 all-reduce.2
  60.4 54.0 all-reduce.4
  116.1 200.3 all-gather.1

commit v2 on v0

--- a/solution.py
+++ b/solution.py
@@ -1,3 +1,4 @@
+import functools
 import jax
 import jax.numpy as jnp
 from jax import lax
@@ -5,6 +6,18 @@
 
 SLAB = 2048
 ridge = 4.0
+
+
+def terms_cover(in_array, row_axis):
+    return jnp.concatenate(
+        lax.all_to_all(
+            jnp.stack(jnp.split(in_array, lax.axis_size(row_axis), axis=1)), row_axis, 0, 0
+        ),
+        axis=0,
+    )
+
+
+plate_register = functools.partial(terms_cover, row_axis="row")
 
 
 def solve_small(matrix, rhs):
@@ -64,7 +77,7 @@
     devices = row_count * col_count
     epochs = rows_dev * devices
     eliminated_own = own_reduced(design, arc_partials, arc_id, arc_weight)
-    regrouped = lax.all_to_all(design, "row", split_axis=1, concat_axis=0, tiled=True)
+    regrouped = plate_register(design)
     columns = lax.all_to_all(eliminated_own, "col", split_axis=1, concat_axis=0, tiled=True)
     slab_global = lax.all_gather(columns, "row", axis=0, tiled=True)
     ordered = col_major(slab_global, row_count, col_count, rows_dev)

time: 401 us -> 389 us (0.970)
  local copies, waits for them, and re-layouts: 34.6 us -> 21.3 us
    mul x1 -> x0, local copies, waits for them, and re-layouts: 23.5 us -> none  [local(): return normal * (1.0 / epochs)]
    unnamed x6 -> x13, local copies, waits for them, and re-layouts: 1.58 us -> 13.8 us
where the time goes in v2:
time: 389 us; the launch traced here: 388 us
  waiting for transfers between devices  250 us (64%)
  blocking collectives  69.1 us (18%)
  local copies, waits for them, and re-layouts  21.3 us (5%)
  between operations  19.5 us (5%)
  matrix products  18.7 us (5%)
  starting transfers between devices  5.42 us (1%)
    psum x1, waiting for transfers between devices, own_reduced(): lax.psum((select[:, None, None] * gram[None], select[:, None, None] * cou...  217 us
    psum x1, blocking collectives, own_reduced(): lax.psum((select[:, None, None] * gram[None], select[:, None, None] * cou...  50.1 us
    all_to_all x1, waiting for transfers between devices, terms_cover(): lax.all_to_all(jnp.stack(jnp.split(in_array, lax.axis_size(row_axis), axi...  33.2 us
    dot_general x1, matrix products, make_accumulate(): lax.dot_general(piece, ordered, (((0,), (0,)), ((), ())), preferred_eleme...  15.7 us
    unnamed x13, local copies, waits for them, and re-layouts  13.8 us
    all_gather x1, blocking collectives, local(): slab_global = lax.all_gather(columns, 'row', axis=0, tiled=True)  9.79 us
    all_to_all x1, blocking collectives, local(): lax.all_to_all(eliminated_own, 'col', split_axis=1, concat_axis=0, tiled=...  9.17 us
  transfers between devices with their start and end apart: 3, of which 2 were waited for; matrix products, arithmetic and copies ran while one was open for 3% of the time, Pallas kernels for 0%

profile of v2, /device:TPU:0, one launch (start us, length us, event | category | flops | bytes accessed | tf_op | source)
XLA Modules:
  0.0 387.7 jit_solution(4442606546653077290)
XLA Ops:
  7.4 1.7 bitcast_dynamic-update-slice_fusion.7
  9.1 1.7 bitcast_dynamic-update-slice_fusion.6
  10.9 1.7 bitcast_dynamic-update-slice_fusion.5
  12.6 1.7 bitcast_dynamic-update-slice_fusion.4
  14.3 1.7 bitcast_dynamic-update-slice_fusion.3
  16.1 1.7 bitcast_dynamic-update-slice_fusion.2
  17.8 1.7 bitcast_dynamic-update-slice_fusion.1
  19.6 1.7 bitcast_dynamic-update-slice_fusion
  21.3 5.3 %all-to-all-start = ((bf16[8,16,11264]{2,1,0:T(8,128)(2,1)}), bf16[8,16,11264]{2,1,0:T(8,128)(2,1)S(1)}, u32[]{:S(2)}, u32[]{:S(2)}) async-start(bf16[8,16,11264]{2,1,0:T(8,128)(2,1)} %bitcast_dynamic-update-slice_fusion), calls=%async_computation | async-start | bytes 5767168 | tf_op jit(solution)/shard_map/all_to_all | solution.py:13
  27.4 1.0 fusion.3
  28.4 0.9 broadcast_multiply_fusion
  29.3 33.2 %all-to-all-done = bf16[8,16,11264]{2,1,0:T(8,128)(2,1)S(1)} async-done(((bf16[8,16,11264]{2,1,0:T(8,128)(2,1)}), bf16[8,16,11264]{2,1,0:T(8,128)(2,1)S(1)}, u32[]{:S(2)}, u32[]{:S(2)}) %all-to-all-start) | async-done | bytes 2883616 | tf_op jit(solution)/shard_map/all_to_all | solution.py:13
  62.5 1.6 copy-done
  64.3 50.1 %psum.15 = f32[8,6,6]{2,0,1:T(8,128)S(1)} all-reduce(f32[8,6,6]{2,0,1:T(8,128)S(1)} %broadcast_multiply_fusion.1), channel_id=1, replica_groups=mesh['row'=8,'col'=4] {'row','col'}, use_global_device_ids=true, to_apply=%region_3.0 | all-reduce | flops 288 | bytes 2304 | tf_op jit(solution)/shard_map/psum | solution.py:45
  114.5 0.5 slice.240
  115.9 0.6 slice.244
  117.4 0.6 slice.248
  119.0 0.6 slice.252
  120.5 0.6 slice.256
  122.1 0.6 slice.260
  123.3 0.7 fusion.12
  124.1 216.6 %all-reduce.2.cloned.1.call-done = f32[8,6,2048]{2,0,1:T(8,128)} async-done(((f32[8,6,2048]{2,0,1:T(8,128)}), f32[8,6,2048]{2,0,1:T(8,128)}) %all-reduce.2.cloned.1.call-update) | async-done | bytes 393232 | tf_op jit(solution)/shard_map/psum | solution.py:45
  340.7 1.2 multiply_reduce_fusion
  342.0 0.2 scatter.36
  342.3 0.2 scatter.40
  342.6 0.2 scatter.44
  342.9 0.2 scatter.46
  343.2 0.2 scatter.50
  343.6 1.8 fusion.2
  345.5 9.2 %all_to_all.24 = bf16[16,4,512]{2,0,1:T(8,128)(2,1)S(1)} all-to-all(bf16[16,4,512]{2,0,1:T(8,128)(2,1)S(1)} %bitcast.76), channel_id=1, replica_groups=mesh['row'=8,'col'=4] {'col'}, dimensions={1} | all-to-all | bytes 131072 | tf_op jit(solution)/shard_map/all_to_all | solution.py:81
  354.7 9.8 %all_gather.7 = bf16[512,512]{1,0:T(8,128)(2,1)S(1)} all-gather(bf16[64,512]{1,0:T(8,128)(2,1)S(1)} %bitcast.75), channel_id=1, replica_groups=mesh['row'=8,'col'=4] {'row'}, dimensions={0}, use_global_device_ids=true | all-gather | bytes 589824 | tf_op jit(solution)/shard_map/all_gather | solution.py:82
  364.5 15.7 %convolution_multiply_fusion = f32[11264,512]{1,0:T(8,128)} fusion(bf16[512,11264]{1,0:T(8,128)(2,1)} %all-gather.2.cloned.1.call-done, bf16[512,512]{1,0:T(8,128)(2,1)S(1)} %bitcast.73), kind=kOutput, calls=%fused_computation | convolution fusion | flops 5911347200 | bytes 35127296 | tf_op jit(solution)/shard_map/dot_general | solution.py:62
  (56 shorter events, 2.8 us)
Async XLA Ops:
  21.3 6.0 %copy-start.1 = (f32[1,6,16]{2,0,1:T(1,128)S(1)}, f32[1,6,16]{2,0,1:T(1,128)}, u32[]{:S(2)}) copy-start(f32[1,6,16]{2,0,1:T(1,128)} %param.27) | copy-start | bytes 1156
  21.3 41.2 %all-to-all-start = ((bf16[8,16,11264]{2,1,0:T(8,128)(2,1)}), bf16[8,16,11264]{2,1,0:T(8,128)(2,1)S(1)}, u32[]{:S(2)}, u32[]{:S(2)}) async-start(bf16[8,16,11264]{2,1,0:T(8,128)(2,1)} %bitcast_dynamic-update-slice_fusion), calls=%async_computation | async-start | bytes 5767168 | tf_op jit(solution)/shard_map/all_to_all | solution.py:13
  26.6 96.6 %copy-start.2 = (f32[8]{0:T(128)S(1)}, f32[8]{0:T(128)}, u32[]{:S(2)}) copy-start(f32[8]{0:T(128)} %param.29) | copy-start | bytes 100
  26.6 314.1 %all-reduce.2.cloned.1.call-start = ((), (), s32[]{:S(2)}) async-start(), calls=%async_computation.3 | async-start | bytes 786432 | tf_op jit(solution)/shard_map/psum | solution.py:45
  29.2 335.3 %all-gather.2.cloned.1.call-start = ((), (), s32[]{:S(2)}) async-start(), calls=%async_computation.2 | async-start | bytes 14417920 | tf_op jit(solution)/shard_map/all_gather | solution.py:84
  62.5 1.6 copy-start
Sparse Core Ops, SparseCore 0:
  32.8 307.9 all-reduce.1
Sparse Core Ops, SparseCore 1:
  64.2 201.6 all-gather.1
